TPU v7x, 256 devices: a whole 4x4x8 slice. The times are simulated.
256 devices in a mesh: coil: 8 (over z_hi, x), ro: 32 (over y, z_lo, core).
Axes of the slice: x: 4, y: 4, z: 8 (z_hi: 2, z_lo: 4; z = z_hi * 4 + z_lo), core: 2. Of those that a mesh axis runs over, the one named last changes fastest.
Arguments:
- kspace: bfloat16 [2, 64, 32, 448, 320], P(None, 'coil', None, 'ro'), may hold values from -884272563206990856199 to 884272563206990856199
- sensitivity: bfloat16 [2, 64, 32, 448, 320], P(None, 'coil', 'ro'), may hold values from -0.75 to 0.75
- sampled: int32 [32, 448], replicated, may hold values 0 or 1
- pole_y: int32 [32, 320], replicated, may hold values from 4 to 112
- order_y: int32 [32, 320], replicated, may hold values from 1 to 3
- pole_z: int32 [32, 448], replicated, may hold values from 4 to 80
- order_z: int32 [32, 448], replicated, may hold values from 1 to 3
Outputs:
- image: float32 [2, 32, 448, 320], P(None, 'ro', 'coil')
All inputs are finite; a program needn't handle non-finite values.
Results may differ from a plain program's by a relative error of at most 0.0056.
Values may be sent and summed in bfloat16 or wider, within the bound.
A program may use at most 128 MiB of HBM per device.

v0:
```python
import math

import jax
import jax.numpy as jnp
from jax import lax
from jax.sharding import PartitionSpec as P


def dft_tables(length):
    index = jnp.arange(length, dtype=jnp.int32)
    product = index[:, None] * index[None, :] % length
    angle = product.astype(jnp.float32) * (2.0 * math.pi / length)
    factor = 1.0 / math.sqrt(length)
    return (
        (jnp.cos(angle) * factor).astype(jnp.bfloat16),
        (jnp.sin(angle) * factor).astype(jnp.bfloat16),
    )


def line_window(frequency, pole, degree):
    quotient = frequency / pole.astype(jnp.float32)
    return 1.0 / (1.0 + jnp.power(quotient, 2.0 * degree.astype(jnp.float32)))


def kz_transform(filtered, kz_cosine, kz_sine):
    real_part, imag_part = (filtered[0], filtered[1])
    hyb_real = jnp.einsum(
        "cakz,zn->cakn", real_part, kz_cosine, preferred_element_type=jnp.float32
    ) - jnp.einsum("cakz,zn->cakn", imag_part, kz_sine, preferred_element_type=jnp.float32)
    hyb_imag = jnp.einsum(
        "cakz,zn->cakn", real_part, kz_sine, preferred_element_type=jnp.float32
    ) + jnp.einsum("cakz,zn->cakn", imag_part, kz_cosine, preferred_element_type=jnp.float32)
    return jnp.stack([hyb_real, hyb_imag]).astype(jnp.bfloat16)


def on_device(kspace, sensitivity, sampled, pole_y, order_y, pole_z, order_z):
    lines_local = kspace.shape[3]
    kz_count = kspace.shape[4]
    ky_count = lines_local * lax.axis_size("ro")
    first_line = lax.axis_index("ro") * lines_local
    kz_cosine, kz_sine = dft_tables(kz_count)
    ky_cosine, ky_sine = dft_tables(ky_count)
    line_index = first_line + jnp.arange(lines_local, dtype=jnp.int32)
    freq_y = jnp.minimum(line_index, ky_count - line_index).astype(jnp.float32)
    col_index = jnp.arange(kz_count, dtype=jnp.int32)
    freq_z = jnp.minimum(col_index, kz_count - col_index).astype(jnp.float32)
    local_sampled = lax.dynamic_slice_in_dim(sampled, first_line, lines_local, 1)
    local_pole_z = lax.dynamic_slice_in_dim(pole_z, first_line, lines_local, 1)
    local_order_z = lax.dynamic_slice_in_dim(order_z, first_line, lines_local, 1)
    weight_y = local_sampled[:, :, None].astype(jnp.float32) * line_window(
        freq_y[None, :, None], pole_y[:, None, :], order_y[:, None, :]
    )
    weight_z = line_window(
        freq_z[None, None, :], local_pole_z[:, :, None], local_order_z[:, :, None]
    )
    filtered = (kspace.astype(jnp.float32) * (weight_y * weight_z)).astype(jnp.bfloat16)
    hybrid = kz_transform(filtered, kz_cosine, kz_sine)
    moved = lax.all_to_all(hybrid, "ro", split_axis=2, concat_axis=3, tiled=True)
    hyb_real, hyb_imag = (moved[0], moved[1])
    img_real = jnp.einsum(
        "nk,cakz->canz", ky_cosine, hyb_real, preferred_element_type=jnp.float32
    ) - jnp.einsum("nk,cakz->canz", ky_sine, hyb_imag, preferred_element_type=jnp.float32)
    img_imag = jnp.einsum(
        "nk,cakz->canz", ky_sine, hyb_real, preferred_element_type=jnp.float32
    ) + jnp.einsum("nk,cakz->canz", ky_cosine, hyb_imag, preferred_element_type=jnp.float32)
    map_real = sensitivity[0]
    map_imag = sensitivity[1]
    out_real = jnp.sum(map_real * img_real + map_imag * img_imag, axis=0)
    out_imag = jnp.sum(map_real * img_imag - map_imag * img_real, axis=0)
    partial_image = jnp.stack([out_real, out_imag])
    return lax.psum_scatter(partial_image, "coil", scatter_dimension=2, tiled=True)


def solution(mesh):
    return jax.shard_map(
        on_device,
        mesh=mesh,
        in_specs=(
            P(None, "coil", None, "ro", None),
            P(None, "coil", "ro", None, None),
            P(),
            P(),
            P(),
            P(),
            P(),
        ),
        out_specs=P(None, "ro", "coil", None),
        check_vma=False,
    )
```

profile of v0, /device:TPU:32, one launch (start us, length us, event | category | flops | bytes accessed | tf_op | source)
XLA Modules:
  0.0 341.2 jit_solution(6022209747926040694)
XLA Ops:
  6.5 0.0 copy-start
  6.5 0.0 all-reduce.3.cloned.1.call-start
  6.6 0.9 constant_dynamic-slice_fusion
  7.4 0.1 copy.64
  7.5 0.1 copy.65
  7.6 0.0 copy-done
  7.6 0.1 constant_dynamic-slice_fusion.2
  7.7 0.1 copy.63
  7.8 0.8 convert_element_type.114
  8.6 0.8 convert_multiply_fusion.4
  9.4 2.3 fusion.15
  11.7 3.8 %multiply_convert_fusion = bf16[2,8,32,14,320]{4,2,3,1,0:T(8,128)(2,1)S(1)} fusion(bf16[2,8,32,14,320]{4,2,3,1,0:T(8,128)(2,1)} %param.7, f32[32,14,320]{2,0,1:T(8,128)S(1)} %fusion.15), kind=kLoop, calls=%fused_computation | loop fusion | flops 6881280 | bytes 9748480 | tf_op jit(solution)/shard_map/convert_element_type | solution.py:56
  15.5 3.4 %fusion.7 = f32[8,32,14,320]{3,1,2,0:T(8,128)S(1)} fusion(bf16[2,8,32,14,320]{4,2,3,1,0:T(8,128)(2,1)S(1)} %multiply_convert_fusion), kind=kOutput, calls=%fused_computation.19 | convolution fusion | flops 735129600 | bytes 7340032 | tf_op jit(solution)/shard_map/cakz,zn->cakn/dot_general | solution.py:27
  18.9 3.4 %fusion.6 = f32[8,32,14,320]{3,1,2,0:T(8,128)S(1)} fusion(bf16[2,8,32,14,320]{4,2,3,1,0:T(8,128)(2,1)S(1)} %multiply_convert_fusion), kind=kOutput, calls=%fused_computation.18 | convolution fusion | flops 735129600 | bytes 7340032 | tf_op jit(solution)/shard_map/cakz,zn->cakn/dot_general | solution.py:30
  22.3 3.8 %fusion.4 = bf16[1,8,32,14,320]{4,2,3,1,0:T(8,128)(2,1)S(1)} fusion(f32[8,32,14,320]{3,1,2,0:T(8,128)S(1)} %fusion.7, bf16[2,8,32,14,320]{4,2,3,1,0:T(8,128)(2,1)S(1)} %multiply_convert_fusion), kind=kOutput, calls=%fused_computation.12 | convolution fusion | flops 737423360 | bytes 10551296 | tf_op jit(solution)/shard_map/cakz,zn->cakn/dot_general | solution.py:29
  26.1 3.6 %fusion.5 = bf16[1,8,32,14,320]{4,2,3,1,0:T(8,128)(2,1)S(1)} fusion(f32[8,32,14,320]{3,1,2,0:T(8,128)S(1)} %fusion.6, bf16[2,8,32,14,320]{4,2,3,1,0:T(8,128)(2,1)S(1)} %multiply_convert_fusion), kind=kOutput, calls=%fused_computation.13 | convolution fusion | flops 737423360 | bytes 10551296 | tf_op jit(solution)/shard_map/cakz,zn->cakn/dot_general | solution.py:32
  29.7 1.1 pad_maximum_fusion
  30.8 3.3 copy.53
  34.1 130.6 %all_to_all.4 = bf16[2,8,32,14,320]{4,1,3,0,2:T(8,128)(2,1)S(1)} all-to-all(bf16[2,8,32,14,320]{4,1,3,0,2:T(8,128)(2,1)S(1)} %copy.53), channel_id=1, replica_groups=mesh['coil'=8,'ro'=32] {'ro'}, dimensions={2} | all-to-all | bytes 9175040 | tf_op jit(solution)/shard_map/all_to_all | solution.py:58
  164.7 3.1 fusion.72
  167.8 3.7 %copy.54 = bf16[8,448,320]{1,2,0:T(8,128)(2,1)S(1)} copy(bf16[8,448,320]{2,0,1:T(8,128)(2,1)} %bitcast.70) | data formatting | bytes 4587520 | tf_op jit(solution)/shard_map/reshape.4
  171.5 8.5 %fusion.26 = f32[8,320,448]{2,1,0:T(8,128)} fusion(bf16[8,448,320]{1,2,0:T(8,128)(2,1)S(1)} %copy.54), kind=kOutput, calls=%fused_computation.51 | convolution fusion | flops 1029812224 | bytes 6881280 | tf_op jit(solution)/shard_map/nk,cakz->canz/dot_general | solution.py:63
  180.1 8.5 %fusion.30 = f32[8,320,448]{2,1,0:T(8,128)} fusion(bf16[8,448,320]{1,2,0:T(8,128)(2,1)S(1)} %copy.54), kind=kOutput, calls=%fused_computation.52 | convolution fusion | flops 1029812224 | bytes 6881280 | tf_op jit(solution)/shard_map/nk,cakz->canz/dot_general | solution.py:60
  188.6 3.7 %copy.55 = bf16[8,448,320]{1,2,0:T(8,128)(2,1)S(1)} copy(bf16[8,448,320]{2,0,1:T(8,128)(2,1)} %bitcast.69) | data formatting | bytes 4587520 | tf_op jit(solution)/shard_map/reshape.9
  192.3 0.0 copy-start.2
  192.3 8.8 %convolution_add_fusion = f32[8,320,448]{2,1,0:T(8,128)S(1)} fusion(f32[8,320,448]{2,1,0:T(8,128)} %fusion.26, bf16[8,448,320]{1,2,0:T(8,128)(2,1)S(1)} %copy.55), kind=kOutput, calls=%fused_computation.20 | convolution fusion | flops 1030959104 | bytes 11468800 | tf_op jit(solution)/shard_map/nk,cakz->canz/dot_general | solution.py:65
  201.1 0.0 copy-done.2
  201.1 0.0 copy-start.1
  201.2 9.9 %fusion.1 = (f32[448,320]{0,1:T(8,128)S(1)}, f32[448,320]{0,1:T(8,128)S(1)}) fusion(f32[8,320,448]{2,1,0:T(8,128)S(1)} %convolution_add_fusion, bf16[2,8,1,448,320]{3,4,1,2,0:T(8,128)(2,1)} %bitcast.73, f32[8,320,448]{2,1,0:T(8,128)S(1)} %copy-done.2, bf16[8,448,320]{1,2,0:T(8,128)(2,1)S(1)} %copy.55), kind=kOutput, calls=%fused_computation.9 | convolution fusion | flops 1042141184 | bytes 17203200 | tf_op jit(solution)/shard_map/nk,cakz->canz/dot_general | solution.py:62
  211.1 0.0 copy-start.3
  211.1 0.1 pad_maximum_fusion.1
  211.2 2.2 copy.59
  213.3 0.0 all-reduce.3.cloned.1.call-update
  213.4 0.0 copy-done.3
  213.4 0.6 dynamic-slice
  214.6 118.1 %all-reduce.3.cloned.1.call-done = f32[2,1,448,320]{3,0,1,2:T(2,128)} async-done(((f32[2,1,448,320]{3,0,1,2:T(2,128)}), f32[2,1,448,320]{3,0,1,2:T(2,128)}) %all-reduce.3.cloned.1.call-update) | async-done | bytes 1146896
  332.7 1.0 constant_dynamic-slice_fusion.3
  333.6 0.7 copy.60
  334.3 0.0 copy-done.1
  (5 shorter events, 0.0 us)
Async XLA Ops:
  6.5 1.1 copy-start
  6.5 326.1 %all-reduce.3.cloned.1.call-start = ((), (), s32[]{:S(2)}) async-start(), calls=%async_computation.1 | async-start | bytes 2752512
  192.3 8.9 %copy-start.2 = (f32[8,320,448]{2,1,0:T(8,128)S(1)}, f32[8,320,448]{2,1,0:T(8,128)}, u32[]{:S(2)}) copy-start(f32[8,320,448]{2,1,0:T(8,128)} %fusion.30) | copy-start | bytes 13762564
  201.1 133.2 %copy-start.1 = (s32[32,448]{1,0:T(8,128)S(1)}, s32[32,448]{1,0:T(8,128)}, u32[]{:S(2)}) copy-start(s32[32,448]{1,0:T(8,128)} %param.9) | copy-start | bytes 172036
  211.1 2.3 copy-start.3
Sparse Core Ops, SparseCore 0:
  213.5 119.1 all-reduce.2
where the time goes:
time: 343 us; the launch traced here: 341 us
  blocking collectives  131 us (38%)
  waiting for transfers between devices  118 us (34%)
  matrix products  50.1 us (15%)
  local copies, waits for them, and re-layouts  19.3 us (6%)
  between operations  14.2 us (4%)
  other arithmetic  8.9 us (3%)
    all_to_all x1, blocking collectives, on_device(): lax.all_to_all(hybrid, 'ro', split_axis=2, concat_axis=3, tiled=True)  131 us
    unnamed x2, waiting for transfers between devices  118 us
    dot_general x1, matrix products, on_device(): jnp.einsum('nk,cakz->canz', ky_sine, hyb_imag, preferred_element_type=jnp...  9.9 us
    dot_general x1, matrix products, on_device(): jnp.einsum('nk,cakz->canz', ky_cosine, hyb_imag, preferred_element_type=j...  8.83 us
    dot_general x1, matrix products, on_device(): jnp.einsum('nk,cakz->canz', ky_sine, hyb_real, preferred_element_type=jnp...  8.54 us
    dot_general x1, matrix products, on_device(): jnp.einsum('nk,cakz->canz', ky_cosine, hyb_real, preferred_element_type=j...  8.52 us
    another operation x2, local copies, waits for them, and re-layouts  7.41 us
  transfers between devices with their start and end apart: 1, of which 1 were waited for; matrix products, arithmetic and copies ran while one was open for 0% of the time, Pallas kernels for 0%

commit v1 on v0

v1 whole, which is shorter than its diff:
```python
import math

import jax
import jax.numpy as jnp
import numpy as np
from jax import lax
from jax.experimental import pallas as pl
from jax.experimental.pallas import tpu as pltpu
from jax.sharding import PartitionSpec as P

MESH = pl.DeviceIdType.MESH
BF16 = jnp.bfloat16
F32 = jnp.float32

NRO = 32
NX = 4
C = 8
LINES = 14
KY = 448
KZ = 320
ROWS = KY // 8
CROWS = 2 * LINES
MROWS = C * CROWS
WIN = 32


def dft_tables(length):
    index = np.arange(length)
    product = (index[:, None] * index[None, :]) % length
    angle = product.astype(np.float32) * np.float32(2.0 * math.pi / length)
    factor = np.float32(1.0 / math.sqrt(length))
    return (
        (np.cos(angle) * factor).astype(BF16).astype(np.float32),
        (np.sin(angle) * factor).astype(BF16).astype(np.float32),
    )


def kz_tables():
    cos, sin = dft_tables(KZ)
    out = np.zeros((2, 4, KZ, 256), np.float32)
    for k in range(2):
        cols = slice(128 * k, 128 * k + 128)
        out[0, k, :, :128], out[0, k, :, 128:] = cos[:, cols], sin[:, cols]
        out[1, k, :, :128], out[1, k, :, 128:] = -sin[:, cols], cos[:, cols]
    for q in range(2):
        re, im = slice(64 * q, 64 * q + 64), slice(128 + 64 * q, 192 + 64 * q)
        cols = slice(256, 320)
        out[0, 2 + q, :, re], out[0, 2 + q, :, im] = cos[:, cols], sin[:, cols]
        out[1, 2 + q, :, re], out[1, 2 + q, :, im] = -sin[:, cols], cos[:, cols]
    return out.astype(BF16)


def ky_tables():
    out = np.zeros((4, KY, 2, 8, 16), np.float32)
    for t, table in enumerate(dft_tables(KY)):
        out[:, :, t, :, :LINES] = table.reshape(KY, 4, 8, LINES).transpose(1, 0, 2, 3)
    return out.reshape(4, KY, 256).astype(BF16)


def partner(t):
    return ((t >> 1) & 3) | ((1 - (t & 1)) << 2) | ((t >> 3) << 3)


def dot(a, b):
    return jnp.dot(a, b, preferred_element_type=F32)


def kernel(
    ks, sens, sampled, pole_y, order_y, pole_z, order_z, kz_tab, ky_tab,
    out,
    kbuf, sraw, smp, py, oy, pz, oz, gtab, ctab,
    wgt, filt, relay, send, send2, recv, recv2, st, st2, wmat, acc, acc2,
    got_a, got_a2, part, part2, got_b, got_b2,
    ksem, lsem, ssem, rsem, sa, ra, sb, rb,
):
    ro = lax.axis_index("ro")
    coil = lax.axis_index("coil")
    x = lax.rem(coil, NX)
    zh = lax.div(coil, NX)

    small = [
        pltpu.make_async_copy(s, d, lsem.at[i])
        for i, (s, d) in enumerate(
            ((sampled, smp), (pole_y, py), (order_y, oy), (pole_z, pz), (order_z, oz))
        )
    ]
    for cp in small:
        cp.start()
    load_g = pltpu.make_async_copy(kz_tab, gtab, lsem.at[5])
    load_k = [
        pltpu.make_async_copy(ks.at[:, c], kbuf.at[:, c], ksem.at[c]) for c in range(C)
    ]
    load_k[0].start()
    load_g.start()
    for c in range(1, C):
        load_k[c].start()
    load_c = pltpu.make_async_copy(ky_tab, ctab, lsem.at[6])
    load_s = pltpu.make_async_copy(sens, sraw, lsem.at[7])
    load_c.start()
    load_s.start()

    barrier = pltpu.get_barrier_semaphore()
    for e in range(1, NRO):
        pl.semaphore_signal(
            barrier, inc=1, device_id={"ro": lax.bitwise_xor(ro, e)}, device_id_type=MESH
        )
    for i in range(1, NX):
        pl.semaphore_signal(
            barrier,
            inc=1,
            device_id={"coil": zh * NX + lax.rem(x + i, NX)},
            device_id_type=MESH,
        )
    pl.semaphore_signal(
        barrier, inc=1, device_id={"coil": (1 - zh) * NX + x}, device_id_type=MESH
    )

    for cp in small:
        cp.wait()
    first = ro * LINES
    lane = lax.broadcasted_iota(jnp.int32, (NRO, KY), 1)
    col = lax.broadcasted_iota(jnp.int32, (NRO, KZ), 1)
    freq_z = jnp.minimum(col, KZ - col).astype(F32)

    def power(quotient, order):
        square = quotient * quotient
        fourth = square * square
        return jnp.where(
            order == 1, square, jnp.where(order == 2, fourth, fourth * square)
        )

    def weigh(j, carry):
        ky = first + j
        freq_y = jnp.minimum(ky, KY - ky).astype(F32)
        here = lane == ky

        def column(ref):
            picked = jnp.where(here, ref[...].astype(F32), 0.0)
            return jnp.sum(picked, axis=1, keepdims=True)

        on = column(smp)
        wy = on / (1.0 + power(freq_y / py[...].astype(F32), oy[...]))
        pole, order = column(pz), column(oz)
        wz = 1.0 / (
            1.0 + power(freq_z / pole, jnp.broadcast_to(order, (NRO, KZ)).astype(jnp.int32))
        )
        wgt[j] = wy * wz
        return carry

    lax.fori_loop(0, LINES, weigh, 0)
    load_g.wait()

    def rows_out(c, value):
        for p in range(2):
            at = pl.multiple_of((2 * c + p) * KY, KY)
            relay[pl.ds(at, KY), :] = value[:, 128 * p : 128 * p + 128]

    def spread(block, at):
        def one(r, carry):
            block[r, at : at + 4 * CROWS, :] = relay[
                pl.ds(r, 4 * CROWS, stride=NRO), :
            ].astype(BF16)
            return carry

        lax.fori_loop(0, NRO, one, 0)

    def send_all(src, dst, k, rows):
        def one(t, carry):
            e = partner(t)

            @pl.when(e != 0)
            def _():
                d = lax.bitwise_xor(ro, e)
                pltpu.make_async_remote_copy(
                    src_ref=src.at[d, rows],
                    dst_ref=dst.at[ro, rows],
                    send_sem=ssem.at[k],
                    recv_sem=rsem.at[k],
                    device_id={"ro": d},
                    device_id_type=MESH,
                ).start()

            return carry

        lax.fori_loop(0, NRO, one, 0)
        pltpu.make_async_copy(src.at[ro, rows], dst.at[ro, rows], rsem.at[k]).start()

    for k in range(2):
        for q in range(2):

            def transform(a, carry):
                c = 4 * q + a
                if k == 0:
                    pltpu.make_async_copy(ks.at[:, c], kbuf.at[:, c], ksem.at[c]).wait()
                    for p in range(2):
                        filt[c, p] = (
                            (kbuf[p, c].astype(F32) * wgt[...])
                            .astype(BF16)
                            .reshape(LINES * NRO, KZ)
                        )
                rows_out(a, dot(filt[c, 0], gtab[0, k]) + dot(filt[c, 1], gtab[1, k]))
                return carry

            lax.fori_loop(0, 4, transform, 0)
            spread(send.at[k], 4 * CROWS * q)
            if k == 0 and q == 0:
                pl.semaphore_wait(barrier, NRO - 1 + NX)
            send_all(send.at[k], recv.at[k], k, pl.ds(4 * CROWS * q, 4 * CROWS))

    def transform2(a, carry):
        rows_out(
            a,
            dot(filt[a, 0], gtab[0, 2])
            + dot(filt[a, 1], gtab[1, 2])
            + dot(filt[4 + a, 0], gtab[0, 3])
            + dot(filt[4 + a, 1], gtab[1, 3]),
        )
        return carry

    lax.fori_loop(0, 4, transform2, 0)
    spread(send2, 0)
    send_all(send2, recv2, 2, pl.ds(0, 4 * CROWS))

    load_c.wait()
    row = lax.broadcasted_iota(jnp.int32, (256, 256), 0)
    colw = lax.broadcasted_iota(jnp.int32, (256, 256), 1)
    same = ((row >> 4) & 7) == (colw >> 5)
    is_sin = (row >> 7) == 1
    line = row & 15
    for e in range(2):
        within = (colw & 31) - 4 * e
        hit = same & (line < LINES)
        real = hit & (within == line)
        imag = hit & (within - LINES == line)
        sel0 = jnp.where(is_sin, -jnp.where(imag, 1.0, 0.0), jnp.where(real, 1.0, 0.0))
        sel1 = jnp.where(is_sin, jnp.where(real, 1.0, 0.0), jnp.where(imag, 1.0, 0.0))
        for g in range(4):
            at = slice(256 * g, 256 * g + 256)
            wmat[e, 0:KY, at] = dot(ctab[g], sel0.astype(BF16)).astype(BF16)
            wmat[e, KY : 2 * KY, at] = dot(ctab[g], sel1.astype(BF16)).astype(BF16)

    load_s.wait()
    eye = (
        lax.broadcasted_iota(jnp.int32, (KY, KY), 0)
        == lax.broadcasted_iota(jnp.int32, (KY, KY), 1)
    )
    eye = jnp.where(eye, 1.0, 0.0).astype(BF16)

    def flip(value):
        return lax.dot_general(
            eye, value, (((1,), (1,)), ((), ())), preferred_element_type=F32
        ).astype(BF16)

    for p in range(2):

        def turn(c, carry):
            st[p, c] = flip(sraw[p, c, 0:256, :])
            return carry

        lax.fori_loop(0, C, turn, 0)

        def turn2(a, carry):
            both = jnp.concatenate(
                [sraw[p, a, 256:KZ, :], sraw[p, 4 + a, 256:KZ, :]], axis=0
            )
            st2[p, a] = flip(both)
            return carry

        lax.fori_loop(0, 4, turn2, 0)

    def window(ref, c):
        at = CROWS * c - 4 * (c % 2)
        return ref[:, at : at + WIN, :].reshape(NRO * WIN, 128)

    def combine(maps, images):
        re = im = None
        for (sr, si), (xr, xi) in zip(maps, images):
            sr, si = sr.astype(F32), si.astype(F32)
            a, b = sr * xr + si * xi, sr * xi - si * xr
            re, im = (a, b) if re is None else (re + a, im + b)
        return re, im

    def ky_pair(ref, e, c0, c1):
        both = jnp.concatenate([window(ref, c0), window(ref, c1)], axis=1)
        value = dot(wmat[e], both)
        return [
            (value[0:KY, 128 * i : 128 * i + 128], value[KY:, 128 * i : 128 * i + 128])
            for i in range(2)
        ]

    def reduce_x(src, dst, k):
        for i in range(1, NX):
            there = lax.rem(x + i, NX)
            pltpu.make_async_remote_copy(
                src_ref=src.at[:, there],
                dst_ref=dst.at[i - 1],
                send_sem=sa.at[k],
                recv_sem=ra.at[k],
                device_id={"coil": zh * NX + there},
                device_id_type=MESH,
            ).start()

    def reduce_z(src, got, total, dst, k):
        pltpu.make_async_copy(got, got, ra.at[k]).wait()
        total[...] = src[:, x] + got[0] + got[1] + got[2]
        pltpu.make_async_remote_copy(
            src_ref=total.at[1 - zh],
            dst_ref=dst,
            send_sem=sb.at[k],
            recv_sem=rb.at[k],
            device_id={"coil": (1 - zh) * NX + x},
            device_id_type=MESH,
        ).start()

    for k in range(2):
        pltpu.make_async_copy(send.at[k], recv.at[k], rsem.at[k]).wait()
        cols = slice(128 * k, 128 * k + 128)
        begun = False
        for e in range(2):
            for m in range(2):
                pair = (4 * m + e, 4 * m + e + 2)
                images = ky_pair(recv.at[k], e, *pair)
                maps = [(st[0, c, :, cols], st[1, c, :, cols]) for c in pair]
                parts = combine(maps, images)
                for g in range(8):
                    for p in range(2):
                        v = parts[p][ROWS * g : ROWS * g + ROWS]
                        if begun:
                            v = v + acc[k, g // NX, g % NX, p]
                        acc[k, g // NX, g % NX, p] = v
                begun = True
        reduce_x(acc.at[k], got_a.at[k], k)
        reduce_z(acc.at[k], got_a.at[k], part.at[k], got_b.at[k], k)

    pltpu.make_async_copy(send2, recv2, rsem.at[2]).wait()
    re = im = None
    for e in range(2):
        images = ky_pair(recv2, e, e, e + 2)
        maps = [(st2[0, a], st2[1, a]) for a in (e, e + 2)]
        a, b = combine(maps, images)
        re, im = (a, b) if re is None else (re + a, im + b)
    low = lax.broadcasted_iota(jnp.int32, (KY, 128), 1) < 64
    both = jnp.where(
        low, re + pltpu.roll(re, 64, 1), im + pltpu.roll(im, 64, 1)
    )
    for g in range(8):
        acc2[g // NX, g % NX] = both[ROWS * g : ROWS * g + ROWS]
    reduce_x(acc2, got_a2, 2)
    reduce_z(acc2, got_a2, part2, got_b2, 2)

    for k in range(2):
        pltpu.make_async_copy(got_b.at[k], got_b.at[k], rb.at[k]).wait()
        out[:, :, 128 * k : 128 * k + 128] = part[k, zh] + got_b[k]
    pltpu.make_async_copy(got_b2, got_b2, rb.at[2]).wait()
    last = part2[zh] + got_b2[...]
    out[0, :, 256:KZ] = last[:, 0:64]
    out[1, :, 256:KZ] = last[:, 64:128]

    for k in range(2):
        sent = send.at[k, pl.ds(0, NRO - 1)]
        pltpu.make_async_copy(sent, sent, ssem.at[k]).wait()
        pltpu.make_async_copy(got_a.at[k], got_a.at[k], sa.at[k]).wait()
        pltpu.make_async_copy(got_b.at[k], got_b.at[k], sb.at[k]).wait()
    sent = send2.at[pl.ds(0, NRO - 1)]
    pltpu.make_async_copy(sent, sent, ssem.at[2]).wait()
    pltpu.make_async_copy(got_a2, got_a2, sa.at[2]).wait()
    pltpu.make_async_copy(got_b2, got_b2, sb.at[2]).wait()


def on_device(kspace, sensitivity, sampled, pole_y, order_y, pole_z, order_z):
    lines_first = jnp.transpose(kspace, (0, 1, 3, 2, 4))
    maps = jnp.transpose(sensitivity[:, :, 0], (0, 1, 3, 2))
    vmem, dma = pltpu.VMEM, pltpu.SemaphoreType.DMA
    anywhere = pl.BlockSpec(memory_space=pl.ANY)
    image = pl.pallas_call(
        kernel,
        out_shape=jax.ShapeDtypeStruct((2, ROWS, KZ), F32),
        in_specs=[anywhere] * 9,
        out_specs=pl.BlockSpec(memory_space=pltpu.VMEM),
        scratch_shapes=[
            vmem((2, C, LINES, NRO, KZ), BF16),
            vmem((2, C, KZ, KY), BF16),
            vmem((NRO, KY), jnp.int32),
            vmem((NRO, KZ), jnp.int32),
            vmem((NRO, KZ), jnp.int32),
            vmem((NRO, KY), jnp.int32),
            vmem((NRO, KY), jnp.int32),
            vmem((2, 4, KZ, 256), BF16),
            vmem((4, KY, 256), BF16),
            vmem((LINES, NRO, KZ), F32),
            vmem((C, 2, LINES * NRO, KZ), BF16),
            vmem((4 * CROWS * NRO, 128), F32),
            vmem((2, NRO, MROWS, 128), BF16),
            vmem((NRO, 4 * CROWS, 128), BF16),
            vmem((2, NRO, MROWS, 128), BF16),
            vmem((NRO, 4 * CROWS, 128), BF16),
            vmem((2, C, KY, 256), BF16),
            vmem((2, 4, KY, 128), BF16),
            vmem((2, 2 * KY, NRO * WIN), BF16),
            vmem((2, 2, NX, 2, ROWS, 128), F32),
            vmem((2, NX, ROWS, 128), F32),
            vmem((2, NX - 1, 2, 2, ROWS, 128), F32),
            vmem((NX - 1, 2, ROWS, 128), F32),
            vmem((2, 2, 2, ROWS, 128), F32),
            vmem((2, ROWS, 128), F32),
            vmem((2, 2, ROWS, 128), F32),
            vmem((ROWS, 128), F32),
            dma((C,)),
            dma((8,)),
            dma((3,)),
            dma((3,)),
            dma((3,)),
            dma((3,)),
            dma((3,)),
            dma((3,)),
        ],
        compiler_params=pltpu.CompilerParams(
            collective_id=0, has_side_effects=True, vmem_limit_bytes=60 * 2**20
        ),
    )(
        lines_first, maps, sampled, pole_y, order_y, pole_z, order_z,
        jnp.asarray(kz_tables()), jnp.asarray(ky_tables()),
    )
    return image[:, None]


def solution(mesh):
    return jax.shard_map(
        on_device,
        mesh=mesh,
        in_specs=(
            P(None, "coil", None, "ro", None),
            P(None, "coil", "ro", None, None),
            P(),
            P(),
            P(),
            P(),
            P(),
        ),
        out_specs=P(None, "ro", "coil", None),
        check_vma=False,
    )
```

time: 343 us -> 131 us (0.38)
  blocking collectives: 131 us -> 0 us
  Pallas kernels: 0 us -> 129 us
  waiting for transfers between devices: 118 us -> 0 us
  matrix products: 50.1 us -> 0 us
  local copies, waits for them, and re-layouts: 19.3 us -> 1.6 us
  between operations: 14.2 us -> 0.01 us
  other arithmetic: 8.9 us -> 0 us
    all_to_all x1 -> x0, blocking collectives: 131 us -> none  [on_device(): lax.all_to_all(hybrid, 'ro', split_axis=2, concat_axis=3, tiled=True)]
    pallas_call x0 -> x1, Pallas kernels: none -> 129 us  [on_device(): pl.pallas_call(kernel, out_shape=jax.ShapeDtypeStruct((2, ROWS, KZ), F32)...]
    unnamed x2 -> x0, waiting for transfers between devices: 118 us -> none
    dot_general x8 -> x0, matrix products: 50.1 us -> none  [the longest x1 9.9 us: on_device(): jnp.einsum('nk,cakz->canz', ky_sine, hyb_imag, preferred_element_type=jnp...]
    another operation x4 -> x0, local copies, waits for them, and re-layouts: 12.9 us -> none
    convert_element_type x6 -> x0, other arithmetic: 4.63 us -> none  [the longest x1 3.79 us: on_device(): (kspace.astype(jnp.float32) * (weight_y * weight_z)).astype(jnp.bfloat16)]
  transfers between devices with their start and end apart: 1 -> 0, of which waited for: 1 -> 0; matrix products, arithmetic and copies ran while one was open for 0% -> 0% of each run, Pallas kernels for 0% -> 0%
where the time goes in v1:
time: 131 us; the launch traced here: 130 us
  Pallas kernels  129 us (98%)
  local copies, waits for them, and re-layouts  1.6 us (1%)
    pallas_call x1, Pallas kernels, on_device(): pl.pallas_call(kernel, out_shape=jax.ShapeDtypeStruct((2, ROWS, KZ), F32)...  129 us

profile of v1, /device:TPU:32, one launch (start us, length us, event | category | flops | bytes accessed | tf_op | source)
XLA Modules:
  0.0 130.4 jit_solution(16699870907491499865)
XLA Ops:
  0.0 128.8 %shard_map.91 = f32[2,56,320]{2,1,0:T(8,128)} custom-call(bf16[2,8,14,32,320]{4,3,2,1,0:T(8,128)(2,1)} %bitcast.7, bf16[2,8,320,448]{3,2,1,0:T(8,128)(2,1)} %bitcast.8, s32[32,448]{1,0:T(8,128)} %sampled.1, s32[32,320]{1,0:T(8,128)} %pole_y.1, s32[32,320]{1,0:T(8,128)} %order_y.1, s32[32,448]{1,0:T(8,128)} %pole_z.1, s32[32,448]{1,0:T(8,128)} %order_z.1, ...), custom_call_target="tpu_custom_call" | custom-call | tf_op jit(solution)/shard_map/pallas_call | solution.py:375
  128.8 1.6 %copy.12 = f32[2,1,56,320]{3,2,1,0:T(8,128)} copy(f32[2,1,56,320]{3,2,1,0:T(8,128)} %bitcast.9) | data formatting | bytes 286720
